TPU v7x, 512 devices: a whole 4x4x16 slice. The times are simulated.
512 devices in a mesh: beam: 16 (over y, x), ma: 32 (over z, core).
Axes of the slice: x: 4, y: 4, z: 16, core: 2. Of those that a mesh axis runs over, the one named last changes fastest.
Arguments:
- sky_harmonics: float32 [64, 2, 2048], P('ma'), may hold values from -6 to 6
- beam_harmonics: float32 [128, 2, 2048], P('beam'), may hold values from -6 to 6
- wigner: bfloat16 [128, 64, 64, 2048], P('beam', 'ma'), may hold values from -0.125 to 0.125
- order_map: int32 [64], replicated, may hold values from 0 to 2047, as said below
- block_owner: int32 [4096, 1], P('ma'), may hold values from 0 to 31; in each aligned block of 128 rows (0 to 127, 128 to 255, ...) at most 8 rows name the same one
- block_local: int32 [4096], P('ma'), may hold values from 0 to 63
- cell_offset: int32 [524288], P('ma'), may hold values from 0 to 126
- cell_fraction: float32 [524288], P('ma'), may hold values from 0 to 1
- beam_angle: float32 [524288], P('ma'), may hold values from -3.140625 to 3.140625
- sample_count: int32 [32], P('ma'), may hold values from 1 to 16384, 393216 in all
- noise_weight: float32 [128, 128], replicated, may hold values from -0.2 to 2, as said below
Outputs:
- sky_gradient: float32 [64, 2, 2048], P('ma', None, 'beam')
Inputs may be any that keep to these rules, and one draw needn't show every extreme that they name: `order_map`: 64 distinct azimuthal orders. `block_owner`: among the 128 sample blocks of one device, at most 8 name the same owner, and in some device some owner is named exactly 8 times. `noise_weight`: diagonal entries lie in 1 to 2, the others within 0.2 in magnitude.
All inputs are finite; a program needn't handle non-finite values. No bound on the sum of `sample_count` on one device may be relied on, other than what follows from the above.
Results may differ from a plain program's by a relative error of at most 0.017.
Values may be sent and summed in bfloat16 or wider, within the bound.
A program may use at most 128 MiB of HBM per device.

v0:
```python
import math
import jax
import jax.numpy as jnp
from jax import lax
from jax.sharding import PartitionSpec as P

PHI = 4096
CELLS = 128


def copy_for_each(array, axis):
    devices = lax.axis_size(axis)
    return lax.all_to_all(
        jnp.broadcast_to(array[None], (devices, *array.shape)), axis, 0, 0, tiled=True
    )


def of_everyone(array, axis):
    return copy_for_each(array, axis).astype(jnp.float32).sum(axis=0)


def split_up(array, dim, devices):
    shape = array.shape
    blocks = array.reshape(*shape[:dim], devices, shape[dim] // devices, *shape[dim + 1 :])
    return jnp.moveaxis(blocks, dim, 0)


def summed_on_arrival(array, axis, dim):
    blocks = split_up(array, dim, lax.axis_size(axis))
    arrived = lax.all_to_all(blocks, axis, split_axis=0, concat_axis=0, tiled=True)
    return arrived.astype(jnp.float32).sum(axis=0)


def cycle_phases(order_map, cycle_cells):
    stepped = jnp.arange(cycle_cells, dtype=jnp.int32)
    phase_turns = order_map[:, None] * stepped[None, :] % cycle_cells
    angles = phase_turns.astype(jnp.float32) * (2.0 * math.pi / cycle_cells)
    scaling = 1.0 / math.sqrt(order_map.shape[0])
    return jnp.stack([jnp.cos(angles), -jnp.sin(angles)], axis=1) * scaling


def rotation(beam_order, beam_angle, total_orders):
    spin_order = ((beam_order + 1) // 2).astype(jnp.float32)
    angles = spin_order * beam_angle
    return jnp.where(beam_order % 2 == 0, jnp.cos(angles), jnp.sin(angles)) / math.sqrt(
        total_orders
    )


def harmonic_product(sky_harmonics, beam_harmonics):
    sky_real = sky_harmonics[None, :, 0]
    sky_imag = sky_harmonics[None, :, 1]
    beam_real = beam_harmonics[:, None, 0]
    beam_imag = beam_harmonics[:, None, 1]
    first = sky_real * beam_real - sky_imag * beam_imag
    second = sky_real * beam_imag + sky_imag * beam_real
    return jnp.stack([first, second], axis=2).astype(jnp.bfloat16)


def gradient_terms(grad_harmonics, beam_harmonics):
    grad_real = grad_harmonics[:, :, 0]
    grad_imag = grad_harmonics[:, :, 1]
    beam_real = beam_harmonics[:, None, 0]
    beam_imag = beam_harmonics[:, None, 1]
    first = jnp.sum(grad_real * beam_real + grad_imag * beam_imag, axis=0)
    second = jnp.sum(grad_imag * beam_real - grad_real * beam_imag, axis=0)
    return jnp.stack([first, second], axis=1)


def interpolate(flat_values, flat_low, fractions):
    return (1.0 - fractions) * flat_values[:, flat_low] + fractions * flat_values[:, flat_low + 1]


def spread(weighted, flat_low, fractions, span_cells):
    blank_grid = jnp.zeros((weighted.shape[0], span_cells), jnp.float32)
    blank_grid = blank_grid.at[:, flat_low].add((1.0 - fractions) * weighted)
    return blank_grid.at[:, flat_low + 1].add(fractions * weighted)


def local(
    sky_harmonics,
    beam_harmonics,
    wigner,
    order_map,
    block_owner,
    block_local,
    cell_offset,
    cell_fraction,
    beam_angle,
    sample_count,
    noise_weight,
):
    highest = lax.Precision.HIGHEST
    ma_count = lax.axis_size("ma")
    beam_count = lax.axis_size("beam")
    local_orders = beam_harmonics.shape[0]
    total_orders = local_orders * beam_count
    cycle_cells = PHI
    block_cells = CELLS
    sample_blocks = block_owner.shape[0]
    capacity = 2 * sample_blocks // ma_count
    cycle_count = wigner.shape[2]
    cycles_local = cycle_count // ma_count
    blocks_local = cycles_local * cycle_cells // block_cells
    product = harmonic_product(sky_harmonics, beam_harmonics)
    cycle_modes = jnp.einsum("kmcl,kmrl->kmcr", product, wigner, preferred_element_type=jnp.float32)
    slab_modes = lax.all_to_all(cycle_modes, "ma", split_axis=3, concat_axis=1, tiled=True)
    phase_table = cycle_phases(order_map, cycle_cells)
    cycle_cube = jnp.einsum("kmcr,mcp->krp", slab_modes, phase_table, precision=highest)
    owners = block_owner[:, 0]
    owner_hot = (owners[:, None] == jnp.arange(ma_count, dtype=jnp.int32)[None, :]).astype(
        jnp.int32
    )
    slot_rank = jnp.sum((jnp.cumsum(owner_hot, axis=0) - owner_hot) * owner_hot, axis=1)
    slot_index = owners * capacity + slot_rank
    requests = jnp.full((ma_count * capacity,), -1, jnp.int32).at[slot_index].set(block_local)
    requests = requests.reshape(ma_count, capacity)
    offsets = cell_offset.reshape(sample_blocks, block_cells)
    fractions = cell_fraction.reshape(sample_blocks, block_cells)
    angles = beam_angle.reshape(sample_blocks, block_cells)
    beam_order = lax.axis_index("beam") * local_orders + jnp.arange(local_orders, dtype=jnp.int32)
    stamps = jnp.arange(sample_blocks * block_cells, dtype=jnp.int32).reshape(
        sample_blocks, block_cells
    )
    valid_mask = (stamps < sample_count[0]).astype(jnp.float32)
    wanted = lax.all_to_all(requests, "ma", split_axis=0, concat_axis=0, tiled=True)
    wanted_flat = wanted.reshape(-1)
    outgoing = jnp.take(
        cycle_cube.reshape(local_orders, blocks_local, block_cells),
        jnp.clip(wanted_flat, 0, blocks_local - 1),
        axis=1,
    )
    outgoing = outgoing * (wanted_flat >= 0).astype(jnp.float32)[None, :, None]
    incoming = lax.all_to_all(
        outgoing.reshape(local_orders, ma_count, capacity, block_cells).astype(jnp.bfloat16),
        "ma",
        split_axis=1,
        concat_axis=1,
        tiled=True,
    ).astype(jnp.float32)
    blocks = jnp.take(
        incoming.reshape(local_orders, ma_count * capacity, block_cells), slot_index, axis=1
    )
    own_low = jnp.arange(sample_blocks, dtype=jnp.int32)[:, None] * block_cells + offsets
    own_turn = rotation(beam_order[:, None, None], angles[None], total_orders)
    values = interpolate(
        blocks.reshape(local_orders, sample_blocks * block_cells), own_low, fractions
    )
    partial_value = jnp.sum(own_turn * values, axis=0)
    signal = (
        of_everyone(partial_value.astype(jnp.bfloat16), "beam").astype(jnp.float32) * valid_mask
    )
    filtered = jnp.einsum("bu,tu->bt", signal, noise_weight, precision=highest) * valid_mask
    weighted = own_turn * filtered[None]
    own_spread = spread(weighted, own_low, fractions, sample_blocks * block_cells)
    own_spread = own_spread.reshape(local_orders, sample_blocks, block_cells)
    back_slots = (
        jnp.zeros((local_orders, ma_count * capacity, block_cells), jnp.float32)
        .at[:, slot_index]
        .set(own_spread)
    )
    arrived = lax.all_to_all(
        back_slots.reshape(local_orders, ma_count, capacity, block_cells).astype(jnp.bfloat16),
        "ma",
        split_axis=1,
        concat_axis=1,
        tiled=True,
    ).astype(jnp.float32)
    chooser = (wanted_flat[None, :] == jnp.arange(blocks_local, dtype=jnp.int32)[:, None]).astype(
        jnp.float32
    )
    cube_grad = jnp.einsum(
        "gs,ksc->kgc",
        chooser,
        arrived.reshape(local_orders, ma_count * capacity, block_cells),
        precision=highest,
    )
    cube_grad = cube_grad.reshape(local_orders, cycles_local, cycle_cells)
    grad_modes = jnp.einsum("krp,mcp->kmcr", cube_grad, phase_table, precision=highest).astype(
        jnp.bfloat16
    )
    grad_cycles = lax.all_to_all(grad_modes, "ma", split_axis=1, concat_axis=3, tiled=True)
    grad_harmonics = jnp.einsum(
        "kmcr,kmrl->kmcl", grad_cycles, wigner, preferred_element_type=jnp.float32
    )
    gradient = gradient_terms(grad_harmonics, beam_harmonics)
    result = summed_on_arrival(gradient.astype(jnp.bfloat16), "beam", 2)
    return result


def solution(mesh):
    return jax.shard_map(
        local,
        mesh=mesh,
        in_specs=(
            P("ma", None, None),
            P("beam", None, None),
            P("beam", "ma", None, None),
            P(),
            P("ma", None),
            P("ma"),
            P("ma"),
            P("ma"),
            P("ma"),
            P("ma"),
            P(),
        ),
        out_specs=P("ma", None, "beam"),
        check_vma=False,
    )
```

profile of v0, /device:TPU:2, one launch (start us, length us, event | category | flops | bytes accessed | tf_op | source)
XLA Modules:
  0.0 597.7 jit_solution(5402851796727341372)
XLA Ops:
  0.0 0.8 fusion.45
  0.8 0.2 reduce_window_sum.11
  1.0 0.8 select_reduce_fusion
  1.8 1.2 and_bitcast_fusion
  3.0 1.1 scatter_custom_fusion
  4.1 0.7 all_to_all.44
  4.8 15.5 %all-to-all-start = ((s32[32,1,8]{2,1,0:T(1,128)}), s32[32,1,8]{2,1,0:T(1,128)S(1)}, u32[]{:S(2)}, u32[]{:S(2)}) async-start(s32[32,1,8]{2,1,0:T(1,128)} %bitcast.12), calls=%async_computation | async-start | bytes 32768 | tf_op jit(solution)/shard_map/all_to_all | solution.py:126
  20.3 1.1 fusion.69
  21.4 0.9 fusion.70
  22.2 4.8 fusion.31
  27.2 0.3 subtract_convert_fusion
  27.5 3.4 fusion.34
  30.8 0.8 copy.89
  31.6 1.1 all-to-all-done
  32.7 11.0 %all-to-all-start.1 = ((f32[8,2,2,64]{0,2,1,3:T(2,128)}), f32[8,2,2,64]{0,2,1,3:T(2,128)S(1)}, u32[]{:S(2)}, u32[]{:S(2)}) async-start(f32[8,2,2,64]{0,2,1,3:T(2,128)} %copy.89), calls=%async_computation.1 | async-start | bytes 262144 | tf_op jit(solution)/shard_map/all_to_all | solution.py:107
  43.8 0.6 broadcast.499
  44.4 1.3 fusion.65
  45.6 0.1 min.18
  45.7 0.6 compare_and_fusion
  46.4 0.6 pad_clamp_fusion.1
  47.0 14.0 %all-to-all-done.1 = f32[8,2,2,64]{0,2,1,3:T(2,128)S(1)} async-done(((f32[8,2,2,64]{0,2,1,3:T(2,128)}), f32[8,2,2,64]{0,2,1,3:T(2,128)S(1)}, u32[]{:S(2)}, u32[]{:S(2)}) %all-to-all-start.1) | async-done | bytes 8224 | tf_op jit(solution)/shard_map/all_to_all | solution.py:107
  61.0 0.1 copy.91
  61.1 1.2 fusion.12
  62.3 1.2 gather_fusion
  63.4 2.1 multiply_convert_fusion
  65.5 4.8 all-to-all-start.2
  70.4 0.6 pad_clamp_fusion
  71.0 0.7 broadcast_bitcast_fusion
  71.7 1.6 broadcast_clamp_fusion
  73.3 30.8 %all-to-all-done.2 = bf16[8,32,8,128]{3,0,2,1:T(8,128)(2,1)} async-done(((bf16[8,32,8,128]{3,0,2,1:T(8,128)(2,1)}), bf16[8,32,8,128]{3,0,2,1:T(8,128)(2,1)}, u32[]{:S(2)}, u32[]{:S(2)}) %all-to-all-start.2) | async-done | bytes 524320 | tf_op jit(solution)/shard_map/all_to_all | solution.py:134
  104.1 1.1 bitcast_convert_fusion
  105.2 1.5 gather_fusion.1
  106.8 5.7 copy.95
  112.4 13.1 %broadcast_select_fusion = f32[8,16384]{0,1:T(8,128)} fusion(f32[8,16384]{0,1:T(8,128)} %copy.95, pred[16384]{0:T(1024)(128)(4,1)S(1)} %broadcast_bitcast_fusion), kind=kLoop, calls=%fused_computation.17 | loop fusion | flops 131072 | bytes 1064960 | tf_op jit(solution)/shard_map/jit(_take)/select_n | solution.py:141
  125.5 57.8 %gather_fusion.2 = f32[16384,8]{1,0:T(8,128)} fusion(f32[8,16384]{0,1:T(8,128)} %broadcast_select_fusion, s32[16384]{0:T(1024)S(1)} %copy-done.7), kind=kCustom, calls=%fused_computation.2 | custom fusion | bytes 1114112 | tf_op jit(solution)/shard_map/gather | solution.py:71
  183.3 57.8 %gather_fusion.3 = f32[16384,8]{1,0:T(8,128)} fusion(f32[8,16384]{0,1:T(8,128)} %broadcast_select_fusion, s32[16384]{0:T(1024)S(1)} %get-tuple-element.11), kind=kCustom, calls=%fused_computation.3 | custom fusion | bytes 1114112 | tf_op jit(solution)/shard_map/gather | solution.py:71
  241.1 39.0 %fusion.6 = bf16[128,128]{1,0:T(8,128)(2,1)S(1)} fusion(f32[128,128,8]{2,1,0:T(8,128)} %bitcast.131, f32[128,128,8]{2,1,0:T(8,128)} %bitcast.130, f32[128,128]{1,0:T(8,128)S(1)} %bitcast.138, f32[128,128]{1,0:T(8,128)S(1)} %broadcast_subtract_fusion, f32[128,128]{1,0:T(8,128)S(1)} %bitcast.142, f32[8]{0:T(128)S(1)} %fusion.56, pred[8]{0:T(512)(128)(4,1)S(1)} %fusion.52), kind=kLoop, calls=%fused_computation.16 | loop fusion | flops 1032192 | bytes 1277992 | tf_op jit(solution)/shard_map/reduce_sum | solution.py:149
  280.1 0.9 broadcast_in_dim.73
  281.0 7.5 %all-to-all-start.3 = ((bf16[16,128,128]{2,1,0:T(8,128)(2,1)}), bf16[16,128,128]{2,1,0:T(8,128)(2,1)S(1)}, u32[]{:S(2)}, u32[]{:S(2)}) async-start(bf16[16,128,128]{2,1,0:T(8,128)(2,1)} %broadcast_in_dim.73), calls=%async_computation.3 | async-start | bytes 1048576 | tf_op jit(solution)/shard_map/all_to_all | solution.py:13
  289.1 9.4 %all-to-all-done.3 = bf16[16,128,128]{2,1,0:T(8,128)(2,1)S(1)} async-done(((bf16[16,128,128]{2,1,0:T(8,128)(2,1)}), bf16[16,128,128]{2,1,0:T(8,128)(2,1)S(1)}, u32[]{:S(2)}, u32[]{:S(2)}) %all-to-all-start.3) | async-done | bytes 524320 | tf_op jit(solution)/shard_map/all_to_all | solution.py:13
  298.5 0.1 convert_reduce_fusion
  298.6 0.3 fusion.14
  298.9 33.4 %fusion.3 = (f32[8,128,128]{0,2,1:T(8,128)}, f32[8,128,128]{0,2,1:T(8,128)}) fusion(f32[128,128]{1,0:T(8,128)S(1)} %fusion.14, f32[128,128]{1,0:T(8,128)S(1)} %bitcast.139, f32[128,128]{1,0:T(8,128)S(1)} %bitcast.143, f32[8]{0:T(128)S(1)} %fusion.56, pred[8]{0:T(512)(128)(4,1)S(1)} %fusion.52, f32[128,128]{1,0:T(8,128)S(1)} %broadcast_subtract_fusion), kind=kLoop, calls=%fused_computation.13 | loop fusion | flops 655360 | bytes 1310760 | tf_op jit(solution)/shard_map/mul | solution.py:77
  332.3 91.3 %scatter_custom_fusion.1 = f32[8,16384]{0,1:T(8,128)} fusion(s32[16384]{0:T(1024)} %get-tuple-element.24, f32[16384,8]{1,0:T(8,128)} %bitcast.132, f32[]{:T(128)} %constant.97.clone.1), kind=kCustom, calls=%fused_computation.18 | custom fusion | flops 131072 | bytes 524800 | tf_op jit(solution)/shard_map/scatter-add | solution.py:76
  423.6 85.3 %scatter_fusion = f32[8,16384]{0,1:T(8,128)} fusion(f32[8,16384]{0,1:T(8,128)} %scatter_custom_fusion.1, s32[16384]{0:T(1024)S(1)} %get-tuple-element.12, f32[16384,8]{1,0:T(8,128)} %bitcast.129), kind=kCustom, calls=%fused_computation.6 | custom fusion | flops 131072 | bytes 1638400 | tf_op jit(solution)/shard_map/scatter-add | solution.py:77
  508.9 5.9 copy.96
  514.8 0.1 broadcast_in_dim.40
  514.9 8.7 %scatter_fusion.1 = f32[8,256,128]{2,0,1:T(8,128)S(1)} fusion(f32[8,256,128]{2,0,1:T(8,128)S(1)} %broadcast_in_dim.40, s32[128]{0:T(128)S(1)} %bitcast.154, f32[128,8,128]{2,1,0:T(8,128)} %bitcast.135), kind=kCustom, calls=%fused_computation.7 | custom fusion | bytes 1573376 | tf_op jit(solution)/shard_map/scatter | solution.py:160
  523.7 0.9 copy.97
  524.5 4.1 all-to-all-start.4
  528.7 0.1 reshape.387
  528.8 33.9 %all-to-all-done.4 = bf16[8,32,8,128]{3,2,0,1:T(8,128)(2,1)S(1)} async-done(((bf16[8,32,8,128]{3,2,0,1:T(8,128)(2,1)}), bf16[8,32,8,128]{3,2,0,1:T(8,128)(2,1)S(1)}, u32[]{:S(2)}, u32[]{:S(2)}) %all-to-all-start.4) | async-done | bytes 524320 | tf_op jit(solution)/shard_map/all_to_all | solution.py:162
  562.6 0.2 convolution_bitcast_fusion
  562.8 0.1 reshape.388
  563.0 2.5 fusion.18
  565.5 0.1 copy.100
  565.7 17.3 %all_to_all.65 = bf16[8,64,2,2]{0,3,2,1:T(2,128)(2,1)S(1)} all-to-all(bf16[8,64,2,2]{0,3,2,1:T(2,128)(2,1)S(1)} %copy.100), channel_id=1, replica_groups=mesh['beam'=16,'ma'=32] {'ma'}, dimensions={1} | all-to-all | bytes 8192 | tf_op jit(solution)/shard_map/all_to_all | solution.py:182
  583.0 0.1 copy.102
  583.1 0.1 copy.103
  583.2 2.8 fusion.71
  586.0 0.3 fusion.68
  586.3 0.2 fusion.39
  586.5 10.5 %all_to_all.66 = bf16[16,2,2,128]{3,1,2,0:T(2,128)(2,1)S(1)} all-to-all(bf16[16,2,2,128]{3,1,2,0:T(2,128)(2,1)S(1)} %maximum_bitcast_fusion), channel_id=1, replica_groups=mesh['beam'=16,'ma'=32] {'beam'}, dimensions={0} | all-to-all | bytes 32768 | tf_op jit(solution)/shard_map/all_to_all | solution.py:30
  597.1 0.6 copy.105
  (35 shorter events, 0.3 us)
Async XLA Ops:
  0.0 298.6 %copy-start = (f32[128,128]{1,0:T(8,128)S(1)}, f32[128,128]{1,0:T(8,128)}, u32[]{:S(2)}) copy-start(f32[128,128]{1,0:T(8,128)} %param.21) | copy-start | bytes 196612
  0.0 71.0 %copy-start.1 = (f32[16384]{0:T(1024)S(1)}, f32[16384]{0:T(1024)}, u32[]{:S(2)}) copy-start(f32[16384]{0:T(1024)} %param.18) | copy-start | bytes 196612
  3.0 18.4 %copy-start.9 = (s32[128,1]{0,1:T(1,128)}, s32[128,1]{0,1:T(1,128)S(1)}, u32[]{:S(2)}) copy-start(s32[128,1]{0,1:T(1,128)S(1)} %get-tuple-element.14) | copy-start | bytes 1540
  4.8 28.0 %all-to-all-start = ((s32[32,1,8]{2,1,0:T(1,128)}), s32[32,1,8]{2,1,0:T(1,128)S(1)}, u32[]{:S(2)}, u32[]{:S(2)}) async-start(s32[32,1,8]{2,1,0:T(1,128)} %bitcast.12), calls=%async_computation | async-start | bytes 32768 | tf_op jit(solution)/shard_map/all_to_all | solution.py:126
  27.1 34.0 %copy-start.2 = (f32[8,2048]{1,0:T(8,128)}, f32[8,2048]{1,0:T(8,128)S(1)}, u32[]{:S(2)}) copy-start(f32[8,2048]{1,0:T(8,128)S(1)} %get-tuple-element.30) | copy-start | bytes 196612
  27.1 34.0 %copy-start.4 = (f32[8,2048]{1,0:T(8,128)}, f32[8,2048]{1,0:T(8,128)S(1)}, u32[]{:S(2)}) copy-start(f32[8,2048]{1,0:T(8,128)S(1)} %get-tuple-element.31) | copy-start | bytes 196612
  32.7 28.2 %all-to-all-start.1 = ((f32[8,2,2,64]{0,2,1,3:T(2,128)}), f32[8,2,2,64]{0,2,1,3:T(2,128)S(1)}, u32[]{:S(2)}, u32[]{:S(2)}) async-start(f32[8,2,2,64]{0,2,1,3:T(2,128)} %copy.89), calls=%async_computation.1 | async-start | bytes 262144 | tf_op jit(solution)/shard_map/all_to_all | solution.py:107
  65.5 38.6 %all-to-all-start.2 = ((bf16[8,32,8,128]{3,0,2,1:T(8,128)(2,1)}), bf16[8,32,8,128]{3,0,2,1:T(8,128)(2,1)}, u32[]{:S(2)}, u32[]{:S(2)}) async-start(bf16[8,32,8,128]{3,0,2,1:T(8,128)(2,1)} %multiply_convert_fusion), calls=%async_computation.2 | async-start | bytes 1048576 | tf_op jit(solution)/shard_map/all_to_all | solution.py:134
  112.4 13.1 %copy-start.7 = (s32[16384]{0:T(1024)S(1)}, s32[16384]{0:T(1024)}, u32[]{:S(2)}) copy-start(s32[16384]{0:T(1024)} %get-tuple-element.23) | copy-start | bytes 196612
  125.5 115.6 %copy-start.6 = (f32[16384]{0:T(1024)S(1)}, f32[16384]{0:T(1024)}, u32[]{:S(2)}) copy-start(f32[16384]{0:T(1024)} %param.19) | copy-start | bytes 196612
  281.0 17.5 %all-to-all-start.3 = ((bf16[16,128,128]{2,1,0:T(8,128)(2,1)}), bf16[16,128,128]{2,1,0:T(8,128)(2,1)S(1)}, u32[]{:S(2)}, u32[]{:S(2)}) async-start(bf16[16,128,128]{2,1,0:T(8,128)(2,1)} %broadcast_in_dim.73), calls=%async_computation.3 | async-start | bytes 1048576 | tf_op jit(solution)/shard_map/all_to_all | solution.py:13
  423.5 91.3 %copy-start.10 = (s32[128,1]{0,1:T(1,128)S(1)}, s32[128,1]{0,1:T(1,128)}, u32[]{:S(2)}) copy-start(s32[128,1]{0,1:T(1,128)} %copy-done.9) | copy-start | bytes 1540
  508.9 19.8 %copy-start.8 = (s32[32,8]{1,0:T(8,128)S(1)}, s32[32,8]{1,0:T(8,128)}, u32[]{:S(2)}) copy-start(s32[32,8]{1,0:T(8,128)} %get-tuple-element.7) | copy-start | bytes 3076
  514.8 71.5 %copy-start.3 = (f32[8,2048]{1,0:T(8,128)S(1)}, f32[8,2048]{1,0:T(8,128)}, u32[]{:S(2)}) copy-start(f32[8,2048]{1,0:T(8,128)} %copy-done.2) | copy-start | bytes 196612
  514.8 71.5 %copy-start.5 = (f32[8,2048]{1,0:T(8,128)S(1)}, f32[8,2048]{1,0:T(8,128)}, u32[]{:S(2)}) copy-start(f32[8,2048]{1,0:T(8,128)} %copy-done.4) | copy-start | bytes 196612
  524.5 38.1 %all-to-all-start.4 = ((bf16[8,32,8,128]{3,2,0,1:T(8,128)(2,1)}), bf16[8,32,8,128]{3,2,0,1:T(8,128)(2,1)S(1)}, u32[]{:S(2)}, u32[]{:S(2)}) async-start(bf16[8,32,8,128]{3,2,0,1:T(8,128)(2,1)} %copy.97), calls=%async_computation.4 | async-start | bytes 1048576 | tf_op jit(solution)/shard_map/all_to_all | solution.py:162
where the time goes:
time: 599 us; the launch traced here: 598 us
  other arithmetic  278 us (46%)
  local copies, waits for them, and re-layouts  148 us (25%)
  waiting for transfers between devices  89.2 us (15%)
  starting transfers between devices  42.9 us (7%)
  blocking collectives  27.8 us (5%)
  matrix products  10.4 us (2%)
    scatter-add x1, other arithmetic, spread(): blank_grid = blank_grid.at[:, flat_low].add((1.0 - fractions) * weighted)  91.3 us
    scatter-add x1, other arithmetic, spread(): return blank_grid.at[:, flat_low + 1].add(fractions * weighted)  85.3 us
    gather x1, local copies, waits for them, and re-layouts, interpolate(): flat_values[:, flat_low + 1]  57.8 us
    gather x1, local copies, waits for them, and re-layouts, interpolate(): flat_values[:, flat_low]  57.8 us
    reduce_sum x1, other arithmetic, local(): partial_value = jnp.sum(own_turn * values, axis=0)  39 us
    all_to_all x1, waiting for transfers between devices, local(): lax.all_to_all(back_slots.reshape(local_orders, ma_count, capacity, block...  33.9 us
    mul x1, other arithmetic, spread(): return blank_grid.at[:, flat_low + 1].add(fractions * weighted)  33.4 us
    all_to_all x1, waiting for transfers between devices, local(): lax.all_to_all(outgoing.reshape(local_orders, ma_count, capacity, block_c...  30.8 us
  transfers between devices with their start and end apart: 5, of which 5 were waited for; matrix products, arithmetic and copies ran while one was open for 3% of the time, Pallas kernels for 0%

commit v1 on v0

--- a/solution.py
+++ b/solution.py
@@ -131,12 +131,22 @@
         axis=1,
     )
     outgoing = outgoing * (wanted_flat >= 0).astype(jnp.float32)[None, :, None]
-    incoming = lax.all_to_all(
-        outgoing.reshape(local_orders, ma_count, capacity, block_cells).astype(jnp.bfloat16),
-        "ma",
-        split_axis=1,
-        concat_axis=1,
-        tiled=True,
+    incoming = jnp.concatenate(
+        lax.all_to_all(
+            jnp.stack(
+                jnp.split(
+                    outgoing.reshape(local_orders, ma_count, capacity, block_cells).astype(
+                        jnp.bfloat16
+                    ),
+                    lax.axis_size("ma"),
+                    axis=1,
+                )
+            ),
+            "ma",
+            0,
+            0,
+        ),
+        axis=1,
     ).astype(jnp.float32)
     blocks = jnp.take(
         incoming.reshape(local_orders, ma_count * capacity, block_cells), slot_index, axis=1

time: 599 us -> 616 us (1.028)
  local copies, waits for them, and re-layouts: 148 us -> 168 us
    unnamed x23 -> x54, local copies, waits for them, and re-layouts: 0.06 us -> 18.7 us
where the time goes in v1:
time: 616 us; the launch traced here: 614 us
  other arithmetic  276 us (45%)
  local copies, waits for them, and re-layouts  168 us (27%)
  waiting for transfers between devices  89.2 us (14%)
  starting transfers between devices  42 us (7%)
  blocking collectives  27.8 us (5%)
  matrix products  10.4 us (2%)
    scatter-add x1, other arithmetic, spread(): blank_grid = blank_grid.at[:, flat_low].add((1.0 - fractions) * weighted)  91.3 us
    scatter-add x1, other arithmetic, spread(): return blank_grid.at[:, flat_low + 1].add(fractions * weighted)  85.3 us
    gather x1, local copies, waits for them, and re-layouts, interpolate(): flat_values[:, flat_low + 1]  57.8 us
    gather x1, local copies, waits for them, and re-layouts, interpolate(): flat_values[:, flat_low]  57.8 us
    reduce_sum x1, other arithmetic, local(): partial_value = jnp.sum(own_turn * values, axis=0)  39 us
    all_to_all x1, waiting for transfers between devices, local(): lax.all_to_all(back_slots.reshape(local_orders, ma_count, capacity, block...  33.9 us
    mul x1, other arithmetic, spread(): return blank_grid.at[:, flat_low + 1].add(fractions * weighted)  33.4 us
    all_to_all x1, waiting for transfers between devices, local(): lax.all_to_all(jnp.stack(jnp.split(outgoing.reshape(local_orders, ma_coun...  30.8 us
  transfers between devices with their start and end apart: 5, of which 5 were waited for; matrix products, arithmetic and copies ran while one was open for 3% of the time, Pallas kernels for 0%

profile of v1, /device:TPU:2, one launch (start us, length us, event | category | flops | bytes accessed | tf_op | source)
XLA Modules:
  0.0 614.5 jit_solution(18272472430506424719)
XLA Ops:
  0.0 0.8 fusion.47
  0.9 0.8 select_reduce_fusion
  1.8 1.2 and_bitcast_fusion
  3.0 1.1 scatter_custom_fusion
  4.1 0.7 all_to_all.44
  4.8 15.5 %all-to-all-start = ((s32[32,1,8]{2,1,0:T(1,128)}), s32[32,1,8]{2,1,0:T(1,128)S(1)}, u32[]{:S(2)}, u32[]{:S(2)}) async-start(s32[32,1,8]{2,1,0:T(1,128)} %bitcast.12), calls=%async_computation | async-start | bytes 32768 | tf_op jit(solution)/shard_map/all_to_all | solution.py:126
  20.3 1.1 fusion.71
  21.4 0.9 fusion.72
  22.3 4.8 fusion.33
  27.5 3.4 fusion.36
  30.8 0.8 copy.192
  31.6 1.1 all-to-all-done
  32.7 11.1 %all-to-all-start.1 = ((f32[8,2,2,64]{0,2,1,3:T(2,128)}), f32[8,2,2,64]{0,2,1,3:T(2,128)S(1)}, u32[]{:S(2)}, u32[]{:S(2)}) async-start(f32[8,2,2,64]{0,2,1,3:T(2,128)} %copy.192), calls=%async_computation.1 | async-start | bytes 262144 | tf_op jit(solution)/shard_map/all_to_all | solution.py:107
  44.4 1.3 fusion.67
  45.7 0.6 compare_and_fusion
  47.0 14.0 %all-to-all-done.1 = f32[8,2,2,64]{0,2,1,3:T(2,128)S(1)} async-done(((f32[8,2,2,64]{0,2,1,3:T(2,128)}), f32[8,2,2,64]{0,2,1,3:T(2,128)S(1)}, u32[]{:S(2)}, u32[]{:S(2)}) %all-to-all-start.1) | async-done | bytes 8224 | tf_op jit(solution)/shard_map/all_to_all | solution.py:107
  61.1 1.2 fusion.12
  62.3 1.2 gather_fusion
  63.5 1.0 fusion.25
  65.0 0.6 constant_dynamic-update-slice_fusion.30
  65.7 0.6 constant_dynamic-update-slice_fusion.29
  66.3 0.6 constant_dynamic-update-slice_fusion.28
  66.9 0.6 constant_dynamic-update-slice_fusion.27
  68.7 0.6 constant_dynamic-update-slice_fusion.24
  70.5 0.6 constant_dynamic-update-slice_fusion.21
  71.1 0.6 constant_dynamic-update-slice_fusion.20
  71.7 0.6 constant_dynamic-update-slice_fusion.19
  72.9 0.6 constant_dynamic-update-slice_fusion.17
  73.5 0.6 constant_dynamic-update-slice_fusion.16
  75.3 0.6 constant_dynamic-update-slice_fusion.13
  75.9 0.6 constant_dynamic-update-slice_fusion.12
  76.5 0.6 constant_dynamic-update-slice_fusion.11
  77.7 0.6 constant_dynamic-update-slice_fusion.9
  78.9 0.6 constant_dynamic-update-slice_fusion.7
  80.1 0.6 constant_dynamic-update-slice_fusion.5
  81.3 0.6 constant_dynamic-update-slice_fusion.3
  83.1 0.6 constant_dynamic-update-slice_fusion
  83.7 4.1 all-to-all-start.2
  87.8 0.6 pad_clamp_fusion
  88.4 0.7 broadcast_bitcast_fusion
  89.2 1.6 broadcast_clamp_fusion
  90.8 30.8 %all-to-all-done.2 = bf16[32,8,1,8,128]{4,3,1,2,0:T(8,128)(2,1)S(1)} async-done(((bf16[32,8,1,8,128]{4,3,1,2,0:T(8,128)(2,1)}), bf16[32,8,1,8,128]{4,3,1,2,0:T(8,128)(2,1)S(1)}, u32[]{:S(2)}, u32[]{:S(2)}) %all-to-all-start.2) | async-done | bytes 524320 | tf_op jit(solution)/shard_map/all_to_all | solution.py:135
  121.6 0.6 copy.200
  122.2 1.5 gather_fusion.1
  123.8 5.7 copy.201
  129.4 13.1 %broadcast_select_fusion = f32[8,16384]{0,1:T(8,128)} fusion(f32[8,16384]{0,1:T(8,128)} %copy.201, pred[16384]{0:T(1024)(128)(4,1)S(1)} %broadcast_bitcast_fusion), kind=kLoop, calls=%fused_computation.17 | loop fusion | flops 131072 | bytes 1064960 | tf_op jit(solution)/shard_map/jit(_take)/select_n | solution.py:151
  142.6 57.8 %gather_fusion.2 = f32[16384,8]{1,0:T(8,128)} fusion(f32[8,16384]{0,1:T(8,128)} %broadcast_select_fusion, s32[16384]{0:T(1024)S(1)} %copy-done.7), kind=kCustom, calls=%fused_computation.2 | custom fusion | bytes 1114112 | tf_op jit(solution)/shard_map/gather | solution.py:71
  200.4 57.8 %gather_fusion.3 = f32[16384,8]{1,0:T(8,128)} fusion(f32[8,16384]{0,1:T(8,128)} %broadcast_select_fusion, s32[16384]{0:T(1024)S(1)} %get-tuple-element.11), kind=kCustom, calls=%fused_computation.3 | custom fusion | bytes 1114112 | tf_op jit(solution)/shard_map/gather | solution.py:71
  258.2 39.0 %fusion.6 = bf16[128,128]{1,0:T(8,128)(2,1)S(1)} fusion(f32[128,128,8]{2,1,0:T(8,128)} %bitcast.260, f32[128,128,8]{2,1,0:T(8,128)} %bitcast.259, f32[128,128]{1,0:T(8,128)S(1)} %bitcast.267, f32[128,128]{1,0:T(8,128)S(1)} %broadcast_subtract_fusion, f32[128,128]{1,0:T(8,128)S(1)} %bitcast.271, f32[8]{0:T(128)S(1)} %fusion.58, pred[8]{0:T(512)(128)(4,1)S(1)} %fusion.54), kind=kLoop, calls=%fused_computation.16 | loop fusion | flops 1032192 | bytes 1277992 | tf_op jit(solution)/shard_map/reduce_sum | solution.py:159
  297.1 0.9 broadcast_in_dim.73
  298.0 7.5 %all-to-all-start.3 = ((bf16[16,128,128]{2,1,0:T(8,128)(2,1)}), bf16[16,128,128]{2,1,0:T(8,128)(2,1)S(1)}, u32[]{:S(2)}, u32[]{:S(2)}) async-start(bf16[16,128,128]{2,1,0:T(8,128)(2,1)} %broadcast_in_dim.73), calls=%async_computation.3 | async-start | bytes 1048576 | tf_op jit(solution)/shard_map/all_to_all | solution.py:13
  306.1 9.4 %all-to-all-done.3 = bf16[16,128,128]{2,1,0:T(8,128)(2,1)S(1)} async-done(((bf16[16,128,128]{2,1,0:T(8,128)(2,1)}), bf16[16,128,128]{2,1,0:T(8,128)(2,1)S(1)}, u32[]{:S(2)}, u32[]{:S(2)}) %all-to-all-start.3) | async-done | bytes 524320 | tf_op jit(solution)/shard_map/all_to_all | solution.py:13
  315.9 33.4 %fusion.3 = (f32[8,128,128]{0,2,1:T(8,128)}, f32[8,128,128]{0,2,1:T(8,128)}) fusion(f32[128,128]{1,0:T(8,128)S(1)} %fusion.14, f32[128,128]{1,0:T(8,128)S(1)} %bitcast.268, f32[128,128]{1,0:T(8,128)S(1)} %bitcast.272, f32[8]{0:T(128)S(1)} %fusion.58, pred[8]{0:T(512)(128)(4,1)S(1)} %fusion.54, f32[128,128]{1,0:T(8,128)S(1)} %broadcast_subtract_fusion), kind=kLoop, calls=%fused_computation.13 | loop fusion | flops 655360 | bytes 1310760 | tf_op jit(solution)/shard_map/mul | solution.py:77
  349.3 91.3 %scatter_custom_fusion.1 = f32[8,16384]{0,1:T(8,128)} fusion(s32[16384]{0:T(1024)} %get-tuple-element.24, f32[16384,8]{1,0:T(8,128)} %bitcast.261, f32[]{:T(128)} %constant.97.clone.1), kind=kCustom, calls=%fused_computation.18 | custom fusion | flops 131072 | bytes 524800 | tf_op jit(solution)/shard_map/scatter-add | solution.py:76
  440.6 85.3 %scatter_fusion = f32[8,16384]{0,1:T(8,128)} fusion(f32[8,16384]{0,1:T(8,128)} %scatter_custom_fusion.1, s32[16384]{0:T(1024)S(1)} %get-tuple-element.12, f32[16384,8]{1,0:T(8,128)} %bitcast.258), kind=kCustom, calls=%fused_computation.6 | custom fusion | flops 131072 | bytes 1638400 | tf_op jit(solution)/shard_map/scatter-add | solution.py:77
  525.9 5.9 copy.202
  531.9 8.7 %scatter_fusion.1 = f32[8,256,128]{2,0,1:T(8,128)S(1)} fusion(f32[8,256,128]{2,0,1:T(8,128)S(1)} %broadcast_in_dim.40, s32[128]{0:T(128)S(1)} %bitcast.283, f32[128,8,128]{2,1,0:T(8,128)} %bitcast.264), kind=kCustom, calls=%fused_computation.7 | custom fusion | bytes 1573376 | tf_op jit(solution)/shard_map/scatter | solution.py:170
  540.7 0.9 copy.203
  541.6 3.9 all-to-all-start.4
  545.6 33.9 %all-to-all-done.4 = bf16[8,32,8,128]{3,2,0,1:T(8,128)(2,1)S(1)} async-done(((bf16[8,32,8,128]{3,2,0,1:T(8,128)(2,1)}), bf16[8,32,8,128]{3,2,0,1:T(8,128)(2,1)S(1)}, u32[]{:S(2)}, u32[]{:S(2)}) %all-to-all-start.4) | async-done | bytes 524320 | tf_op jit(solution)/shard_map/all_to_all | solution.py:172
  579.8 2.5 fusion.18
  582.5 17.3 %all_to_all.65 = bf16[8,64,2,2]{0,3,2,1:T(2,128)(2,1)S(1)} all-to-all(bf16[8,64,2,2]{0,3,2,1:T(2,128)(2,1)S(1)} %copy.206), channel_id=1, replica_groups=mesh['beam'=16,'ma'=32] {'ma'}, dimensions={1} | all-to-all | bytes 8192 | tf_op jit(solution)/shard_map/all_to_all | solution.py:192
  600.0 2.8 fusion.73
  603.3 10.5 %all_to_all.66 = bf16[16,2,2,128]{3,1,2,0:T(2,128)(2,1)S(1)} all-to-all(bf16[16,2,2,128]{3,1,2,0:T(2,128)(2,1)S(1)} %maximum_bitcast_fusion), channel_id=1, replica_groups=mesh['beam'=16,'ma'=32] {'beam'}, dimensions={0} | all-to-all | bytes 32768 | tf_op jit(solution)/shard_map/all_to_all | solution.py:30
  (68 shorter events, 12.7 us)
Async XLA Ops:
  0.0 315.6 %copy-start = (f32[128,128]{1,0:T(8,128)S(1)}, f32[128,128]{1,0:T(8,128)}, u32[]{:S(2)}) copy-start(f32[128,128]{1,0:T(8,128)} %param.21) | copy-start | bytes 196612
  3.0 18.4 %copy-start.9 = (s32[128,1]{0,1:T(1,128)}, s32[128,1]{0,1:T(1,128)S(1)}, u32[]{:S(2)}) copy-start(s32[128,1]{0,1:T(1,128)S(1)} %get-tuple-element.14) | copy-start | bytes 1540
  4.8 28.0 %all-to-all-start = ((s32[32,1,8]{2,1,0:T(1,128)}), s32[32,1,8]{2,1,0:T(1,128)S(1)}, u32[]{:S(2)}, u32[]{:S(2)}) async-start(s32[32,1,8]{2,1,0:T(1,128)} %bitcast.12), calls=%async_computation | async-start | bytes 32768 | tf_op jit(solution)/shard_map/all_to_all | solution.py:126
  21.4 67.0 %copy-start.1 = (f32[16384]{0:T(1024)S(1)}, f32[16384]{0:T(1024)}, u32[]{:S(2)}) copy-start(f32[16384]{0:T(1024)} %param.18) | copy-start | bytes 196612
  27.1 34.0 %copy-start.2 = (f32[8,2048]{1,0:T(8,128)}, f32[8,2048]{1,0:T(8,128)S(1)}, u32[]{:S(2)}) copy-start(f32[8,2048]{1,0:T(8,128)S(1)} %get-tuple-element.30) | copy-start | bytes 196612
  27.1 34.0 %copy-start.4 = (f32[8,2048]{1,0:T(8,128)}, f32[8,2048]{1,0:T(8,128)S(1)}, u32[]{:S(2)}) copy-start(f32[8,2048]{1,0:T(8,128)S(1)} %get-tuple-element.31) | copy-start | bytes 196612
  32.7 28.3 %all-to-all-start.1 = ((f32[8,2,2,64]{0,2,1,3:T(2,128)}), f32[8,2,2,64]{0,2,1,3:T(2,128)S(1)}, u32[]{:S(2)}, u32[]{:S(2)}) async-start(f32[8,2,2,64]{0,2,1,3:T(2,128)} %copy.192), calls=%async_computation.1 | async-start | bytes 262144 | tf_op jit(solution)/shard_map/all_to_all | solution.py:107
  83.7 37.9 %all-to-all-start.2 = ((bf16[32,8,1,8,128]{4,3,1,2,0:T(8,128)(2,1)}), bf16[32,8,1,8,128]{4,3,1,2,0:T(8,128)(2,1)S(1)}, u32[]{:S(2)}, u32[]{:S(2)}) async-start(bf16[32,8,1,8,128]{4,3,1,2,0:T(8,128)(2,1)} %constant_dynamic-update-slice_fusion), calls=%async_computation.2 | async-start | bytes 1048576 | tf_op jit(solution)/shard_map/all_to_all | solution.py:135
  129.4 13.1 %copy-start.7 = (s32[16384]{0:T(1024)S(1)}, s32[16384]{0:T(1024)}, u32[]{:S(2)}) copy-start(s32[16384]{0:T(1024)} %get-tuple-element.23) | copy-start | bytes 196612
  142.6 115.6 %copy-start.6 = (f32[16384]{0:T(1024)S(1)}, f32[16384]{0:T(1024)}, u32[]{:S(2)}) copy-start(f32[16384]{0:T(1024)} %param.19) | copy-start | bytes 196612
  298.0 17.5 %all-to-all-start.3 = ((bf16[16,128,128]{2,1,0:T(8,128)(2,1)}), bf16[16,128,128]{2,1,0:T(8,128)(2,1)S(1)}, u32[]{:S(2)}, u32[]{:S(2)}) async-start(bf16[16,128,128]{2,1,0:T(8,128)(2,1)} %broadcast_in_dim.73), calls=%async_computation.3 | async-start | bytes 1048576 | tf_op jit(solution)/shard_map/all_to_all | solution.py:13
  440.6 91.3 %copy-start.10 = (s32[128,1]{0,1:T(1,128)S(1)}, s32[128,1]{0,1:T(1,128)}, u32[]{:S(2)}) copy-start(s32[128,1]{0,1:T(1,128)} %copy-done.9) | copy-start | bytes 1540
  525.9 19.6 %copy-start.8 = (s32[32,8]{1,0:T(8,128)S(1)}, s32[32,8]{1,0:T(8,128)}, u32[]{:S(2)}) copy-start(s32[32,8]{1,0:T(8,128)} %get-tuple-element.7) | copy-start | bytes 3076
  531.8 71.3 %copy-start.3 = (f32[8,2048]{1,0:T(8,128)S(1)}, f32[8,2048]{1,0:T(8,128)}, u32[]{:S(2)}) copy-start(f32[8,2048]{1,0:T(8,128)} %copy-done.2) | copy-start | bytes 196612
  531.8 71.3 %copy-start.5 = (f32[8,2048]{1,0:T(8,128)S(1)}, f32[8,2048]{1,0:T(8,128)}, u32[]{:S(2)}) copy-start(f32[8,2048]{1,0:T(8,128)} %copy-done.4) | copy-start | bytes 196612
  541.6 37.9 %all-to-all-start.4 = ((bf16[8,32,8,128]{3,2,0,1:T(8,128)(2,1)}), bf16[8,32,8,128]{3,2,0,1:T(8,128)(2,1)S(1)}, u32[]{:S(2)}, u32[]{:S(2)}) async-start(bf16[8,32,8,128]{3,2,0,1:T(8,128)(2,1)} %copy.203), calls=%async_computation.4 | async-start | bytes 1048576 | tf_op jit(solution)/shard_map/all_to_all | solution.py:172
